TPU v7x, 256 devices: a whole 4x4x8 slice. The times are simulated.
256 devices in a mesh: dp: 8 (over z_lo, x), seq: 32 (over y, z_hi, core).
Axes of the slice: x: 4, y: 4, z: 8 (z_hi: 4, z_lo: 2; z = z_hi * 2 + z_lo), core: 2. Of those that a mesh axis runs over, the one named last changes fastest.
Arguments:
- queries: bfloat16 [8, 4096, 4096], P('dp', 'seq'), may hold values from -5 to 5
- rotated_key_rows: bfloat16 [8, 4096, 512], P('dp', 'seq'), may hold values from -5 to 5
- hidden_states: bfloat16 [8, 4096, 8192], P('dp', 'seq'), may hold values from -6 to 6
- block_order: int32 [64], replicated, may hold values from 0 to 63, each once
- first_weight: bfloat16 [8192, 512], replicated, may hold values from -0.0625 to 0.0625
- first_bias: float32 [512], replicated, may hold values from -3 to 3
- output_weight: bfloat16 [4, 512], replicated, may hold values from -0.25 to 0.25
- output_bias: float32 [4], replicated, may hold values from -1 to 1
Outputs:
- token_attention_mass: float32 [8, 4, 4096], P('dp', None, 'seq')
- loss_value: float32 [], replicated
- step_first: float32 [8192, 512], P('seq')
- output_weight_step: float32 [4, 512], replicated
- step_bias: float32 [512], replicated
- grad_bias: float32 [4], replicated
All inputs are finite; a program needn't handle non-finite values.
Results may differ from a plain program's by a relative error of at most 0.0023.
Values may be sent and summed in bfloat16 or wider, within the bound.
A program may use at most 64 MiB of HBM per device.

v0:
```python
import math
import jax
import jax.numpy as jnp
from jax import lax
from jax.sharding import PartitionSpec as P

D = 8192
KEY_VALUE_HEADS = 4
HEAD_SIZE = 128
RETAIN_HIDDEN = 512
BLK = 64
QUERY_GROUP_SIZE = 8


def key_places(block_order, offset, amount):
    row_ids = offset + lax.iota(jnp.int32, amount)
    block_ids = row_ids // BLK
    block_table = lax.iota(jnp.int32, block_order.shape[0])
    anchor = jnp.sum(
        jnp.where(block_ids[:, None] == block_table[None, :], block_order[None, :], 0), axis=1
    )
    return anchor * BLK + row_ids % BLK


def raw_scores(head_queries, mass_portion):
    head_keys = mass_portion.reshape(mass_portion.shape[0], KEY_VALUE_HEADS, HEAD_SIZE)
    return jnp.einsum(
        "tkgd,nkd->kgtn", head_queries, head_keys, preferred_element_type=jnp.float32
    ) * HEAD_SIZE ** (-0.5)


def blockwise(mass_portion, offset, update, carried):
    rows_here = mass_portion.shape[0]
    inner = math.gcd(rows_here, BLK)

    def visit_block(step_index, running):
        local_start = step_index * inner
        sub_rows = lax.dynamic_slice_in_dim(mass_portion, local_start, inner, 0)
        return update(running, sub_rows, offset + local_start)

    return lax.fori_loop(0, rows_here // inner, visit_block, carried)


def normalizer_step(running, mass_portion, key_start, head_queries, query_pos, block_order):
    highest, summed = running
    key_pos = key_places(block_order, key_start, mass_portion.shape[0])

    def normalizer_compute_step():
        scores = raw_scores(head_queries, mass_portion)
        visible = query_pos[:, None] >= key_pos[None, :]
        masked = jnp.where(visible, scores, -1e30)
        raised = jnp.maximum(highest, jnp.max(masked, axis=-1))
        exponents = jnp.where(visible, jnp.exp(masked - raised[..., None]), 0.0)
        return (raised, summed * jnp.exp(highest - raised) + jnp.sum(exponents, axis=-1))

    return lax.cond(
        jnp.min(key_pos) > jnp.max(query_pos), lambda: (highest, summed), normalizer_compute_step
    )


def mass_step(mass_portion, key_start, head_queries, query_pos, log_total, block_order):
    amount = mass_portion.shape[0]
    key_pos = key_places(block_order, key_start, amount)

    def mass_compute_step():
        scores = raw_scores(head_queries, mass_portion)
        visible = query_pos[:, None] >= key_pos[None, :]
        masked = jnp.where(visible, scores, -1e30)
        weights = jnp.where(visible, jnp.exp(masked - log_total[..., None]), 0.0)
        return jnp.sum(weights, axis=(1, 2)) / QUERY_GROUP_SIZE

    return lax.cond(
        jnp.min(key_pos) > jnp.max(query_pos),
        lambda: jnp.zeros((KEY_VALUE_HEADS, amount), jnp.float32),
        mass_compute_step,
    )


def normalized_scores(value_rows, square_sum, entries):
    return value_rows / jnp.sqrt(square_sum / entries + 1e-06)


def per_device(
    queries,
    rotated_key_rows,
    hidden_states,
    block_order,
    first_weight,
    first_bias,
    output_weight,
    output_bias,
):
    local_row_slice = queries.shape[1]
    total_length = local_row_slice * lax.axis_size("seq")
    head_queries = queries.reshape(local_row_slice, KEY_VALUE_HEADS, QUERY_GROUP_SIZE, HEAD_SIZE)
    local_key_rows = rotated_key_rows.reshape(local_row_slice, KEY_VALUE_HEADS * HEAD_SIZE)
    query_pos = key_places(block_order, lax.axis_index("seq") * local_row_slice, local_row_slice)
    start_state = (
        jnp.full((KEY_VALUE_HEADS, QUERY_GROUP_SIZE, local_row_slice), -1e30, jnp.float32),
        jnp.zeros((KEY_VALUE_HEADS, QUERY_GROUP_SIZE, local_row_slice), jnp.float32),
    )

    def norm_update(running, sub_rows, key_start):
        return normalizer_step(running, sub_rows, key_start, head_queries, query_pos, block_order)

    empty_mass = jnp.zeros((KEY_VALUE_HEADS, total_length), jnp.float32)
    keys_whole = lax.all_gather(local_key_rows, "seq", axis=0, tiled=True)
    highest, summed = blockwise(keys_whole, 0, norm_update, start_state)
    log_total = highest + jnp.log(summed)

    def add_kept(collected, sub_rows, key_start):
        term = mass_step(sub_rows, key_start, head_queries, query_pos, log_total, block_order)
        return lax.dynamic_update_slice_in_dim(collected, term, key_start, 1)

    column_mass = blockwise(keys_whole, 0, add_kept, empty_mass)
    key_attention_mass = lax.psum_scatter(column_mass, "seq", scatter_dimension=1, tiled=True)
    tokens_in = hidden_states.reshape(local_row_slice, hidden_states.shape[2])
    pre_act = jnp.dot(tokens_in, first_weight, preferred_element_type=jnp.float32) + first_bias
    hidden = jax.nn.silu(pre_act).astype(jnp.bfloat16)
    predicted_scores = (
        lax.dot_general(
            output_weight, hidden, (((1,), (1,)), ((), ())), preferred_element_type=jnp.float32
        )
        + output_bias[:, None]
    )
    score_residue = predicted_scores - jnp.log(1.0 + key_attention_mass)
    loss_part = 0.5 * jnp.sum(score_residue * score_residue) / total_length
    out_grad = score_residue / total_length
    bias_part = jnp.sum(out_grad, axis=1)
    second_part = jnp.dot(out_grad, hidden.astype(jnp.float32), precision=lax.Precision.HIGHEST)
    back_grad = jnp.dot(
        out_grad.T, output_weight.astype(jnp.float32), precision=lax.Precision.HIGHEST
    )
    gate_value = jax.nn.sigmoid(pre_act)
    slope_grad = back_grad * gate_value * (1.0 + pre_act * (1.0 - gate_value))
    first_bias_part = jnp.sum(slope_grad, axis=0)
    slope_half = slope_grad.astype(jnp.bfloat16)
    columns_all = lax.all_to_all(tokens_in, "seq", split_axis=1, concat_axis=0, tiled=True)
    slope_all = lax.all_gather(slope_half, "seq", axis=0, tiled=True)
    first_shard = lax.dot_general(
        columns_all, slope_all, (((0,), (0,)), ((), ())), preferred_element_type=jnp.float32
    )
    output_total, first_bias_total, bias_total, loss_total = lax.psum(
        (second_part, first_bias_part, bias_part, loss_part), ("dp", "seq")
    )
    first_grad = lax.psum(first_shard, "dp")
    first_square = lax.psum(jnp.sum(first_grad * first_grad), "seq")
    step_first = normalized_scores(first_grad, first_square, D * RETAIN_HIDDEN)
    output_weight_step = normalized_scores(
        output_total, jnp.sum(output_total * output_total), RETAIN_HIDDEN * KEY_VALUE_HEADS
    )
    step_bias = normalized_scores(
        first_bias_total, jnp.sum(first_bias_total * first_bias_total), RETAIN_HIDDEN
    )
    return (
        key_attention_mass.reshape(1, KEY_VALUE_HEADS, local_row_slice),
        loss_total,
        step_first,
        output_weight_step,
        step_bias,
        bias_total,
    )


def solution(mesh):
    in_specs = (
        P("dp", "seq", None),
        P("dp", "seq", None),
        P("dp", "seq", None),
        P(),
        P(),
        P(),
        P(),
        P(),
    )
    out_specs = (P("dp", None, "seq"), P(), P("seq", None), P(), P(), P())
    return jax.shard_map(
        per_device, mesh=mesh, in_specs=in_specs, out_specs=out_specs, check_vma=False
    )
```

profile of v0, /device:TPU:1, one launch (start us, length us, event | category | flops | bytes accessed | tf_op | source)
XLA Modules:
  0.0 925.9 jit_solution(2229353486682803280)
XLA Ops:
  11.0 64.1 %all-gather.6.cloned.1.call-done = bf16[1,4096,512]{2,1,0:T(8,128)(2,1)} async-done(((bf16[1,128,512]{2,1,0:T(8,128)(2,1)}), bf16[1,4096,512]{2,1,0:T(8,128)(2,1)}) %all-gather.6.cloned.1.call-update) | async-done | bytes 4194320 | tf_op jit(solution)/shard_map/all_gather | solution.py:107
  75.1 206.3 %while.32 = (s32[]{:T(128)}, f32[4,8,128]{2,1,0:T(8,128)S(1)}, f32[4,8,128]{2,1,0:T(8,128)S(1)}, s32[64]{0:T(128)S(1)}, s32[]{:T(128)}, /*index=5*/s32[128]{0:T(...) while((s32[]{:T(128)}, f32[4,8,128]{2,1,0:T(8,128)S(1)}, ...), condition=%wide.region_9.10_spmd, body=%wide.region_2.9_spmd.sunk | while | flops 68712320 | bytes 3713545 | solution.py:41
  83.4 1.7 conditional.4
  87.3 1.7 conditional.4
  156.9 1.7 conditional.4
  173.1 1.7 conditional.4
  184.9 1.7 conditional.4
  199.3 1.7 conditional.4
  221.6 1.7 conditional.4
  235.6 1.7 conditional.4
  239.5 1.7 conditional.4
  269.1 1.7 conditional.4
  281.5 212.6 %while.33 = (s32[]{:T(128)}, f32[4,4096]{1,0:T(4,128)S(1)}, s32[64]{0:T(128)S(1)}, s32[]{:T(128)}, s32[128]{0:T(128)S(1)}, /*index=5*/bf16[4096,512]{1,0:T(8,128...) while((s32[]{:T(128)}, f32[4,4096]{1,0:T(4,128)S(1)}, ...), condition=%wide.region_16.17_spmd, body=%wide.region_10.16_spmd.sunk | while | flops 68441992 | bytes 1416701 | solution.py:41
  494.1 2.0 copy.51
  496.2 4.8 multiply_convert_fusion
  501.0 164.5 %reduce-scatter.4.cloned.1.call-done = f32[128,4]{1,0:T(8,128)} async-done(((f32[4096,4]{1,0:T(8,128)}), f32[128,4]{1,0:T(8,128)}) %reduce-scatter.4.cloned.1.call-update) | async-done | bytes 2064
  668.3 2.5 copy.42
  670.8 63.7 %all_to_all.19 = bf16[128,32,256]{0,2,1:T(8,128)(2,1)S(1)} all-to-all(bf16[128,32,256]{0,2,1:T(8,128)(2,1)} %bitcast.50), channel_id=1, replica_groups=mesh['dp'=8,'seq'=32] {'seq'}, dimensions={1} | all-to-all | bytes 4194304 | tf_op jit(solution)/shard_map/all_to_all | solution.py:138
  734.5 2.9 copy.43
  737.4 19.9 %all-gather.4.cloned.1.call-done = bf16[4096,512]{1,0:T(8,128)(2,1)} async-done(((bf16[128,512]{1,0:T(8,128)(2,1)}), bf16[4096,512]{1,0:T(8,128)(2,1)}) %all-gather.4.cloned.1.call-update) | async-done | bytes 4194320 | tf_op jit(solution)/shard_map/all_gather | solution.py:139
  757.3 4.9 convolution_bitcast_fusion
  763.1 77.0 %all-reduce = (f32[]{:T(128)}, f32[4,512]{1,0:T(4,128)S(1)}, f32[512]{0:T(512)S(1)}, f32[4]{0:T(128)}) all-reduce(f32[]{:T(128)S(6)} %div.87, f32[4,512]{1,0:T(4,128)S(1)} %fusion.20, f32[512]{0:T(512)S(1)} %get-tuple-element.630, f32[4]{0:T(128)S(1)} %get-tuple-element.583), channel_id=1, replica_groups=mesh['dp'=8,'seq'=32] {'dp','seq'}, use_global_device_ids=true, to_apply=%region_19.20 | all-reduce | flops 2565 | bytes 20520 | tf_op jit(solution)/shard_map/psum | solution.py:143
  843.3 1.8 multiply_reduce_fusion
  845.7 70.9 %psum.44 = f32[]{:T(128)} all-reduce(f32[]{:T(128)} %multiply_reduce_fusion), channel_id=1, replica_groups=mesh['dp'=8,'seq'=32] {'seq'}, use_global_device_ids=true, to_apply=%region_22.23 | all-reduce | flops 1 | bytes 8 | tf_op jit(solution)/shard_map/psum | solution.py:147
  (1178 shorter events, 364.6 us)
Async XLA Ops:
  7.2 659.3 %copy-start = (bf16[4,512]{1,0:T(4,128)(2,1)S(1)}, bf16[4,512]{1,0:T(4,128)(2,1)}, u32[]{:S(2)}) copy-start(bf16[4,512]{1,0:T(4,128)(2,1)} %param.22) | copy-start | bytes 12292
  7.2 3.1 copy-start.4
  7.2 67.9 %all-gather.6.cloned.1.call-start = ((), (), s32[]{:S(2)}) async-start(), calls=%async_computation.4 | async-start | bytes 4325376 | tf_op jit(solution)/shard_map/all_gather | solution.py:107
  7.9 657.6 %reduce-scatter.4.cloned.1.call-start = ((), (), s32[]{:S(2)}) async-start(), calls=%async_computation.5 | async-start | bytes 2162688
  494.1 2.1 copy-start.1
  494.1 2.1 copy-start.2
  496.1 170.4 %copy-start.5 = (f32[4]{0:T(128)S(1)}, f32[4]{0:T(128)}, u32[]{:S(2)}) copy-start(f32[4]{0:T(128)} %param.23) | copy-start | bytes 52
  496.1 261.2 %all-gather.4.cloned.1.call-start = ((), (), s32[]{:S(2)}) async-start(), calls=%async_computation.2 | async-start | bytes 4325376 | tf_op jit(solution)/shard_map/all_gather | solution.py:139
  666.4 68.1 %copy-start.3 = (f32[4,128]{1,0:T(4,128)}, f32[4,128]{1,0:T(4,128)S(1)}, u32[]{:S(2)}) copy-start(f32[4,128]{1,0:T(4,128)S(1)} %copy.52) | copy-start | bytes 6148
  668.2 175.1 %all-reduce.3.cloned.1.call-start = ((), (), s32[]{:S(2)}) async-start(), calls=%async_computation.3 | async-start | bytes 1048576 | tf_op jit(solution)/shard_map/psum | solution.py:146
Sparse Core Ops, SparseCore 0:
  10.6 64.5 all-gather.5
  496.2 169.2 reduce-scatter.3
  668.7 88.6 all-gather.3
  762.4 72.5 all-reduce.2
where the time goes:
time: 935 us; the launch traced here: 926 us
  waiting for transfers between devices  249 us (27%)
  blocking collectives  212 us (23%)
  loops' own time  175 us (19%)
  other arithmetic  128 us (14%)
  local copies, waits for them, and re-layouts  92.1 us (10%)
  matrix products  52.9 us (6%)
  between operations  16.7 us (2%)
    another operation x2, loops' own time, blockwise(): return lax.fori_loop(0, rows_here // inner, visit_block, carried)  171 us
    unnamed x5, waiting for transfers between devices  165 us
    psum x1, blocking collectives, per_device(): lax.psum((second_part, first_bias_part, bias_part, loss_part), ('dp', 'se...  77 us
    psum x1, blocking collectives, per_device(): first_square = lax.psum(jnp.sum(first_grad * first_grad), 'seq')  70.9 us
    dynamic_slice x76, local copies, waits for them, and re-layouts, visit_block(): sub_rows = lax.dynamic_slice_in_dim(mass_portion, local_start, inner, 0)  64.7 us
    all_gather x1, waiting for transfers between devices, per_device(): keys_whole = lax.all_gather(local_key_rows, 'seq', axis=0, tiled=True)  64.1 us
    all_to_all x1, blocking collectives, per_device(): lax.all_to_all(tokens_in, 'seq', split_axis=1, concat_axis=0, tiled=True)  63.7 us
    reduce_min x64, other arithmetic, normalizer_step(): jnp.min(key_pos) > jnp.max(query_pos)  41.8 us
  transfers between devices with their start and end apart: 4, of which 3 were waited for; matrix products, arithmetic and copies ran while one was open for 2% of the time, Pallas kernels for 0%

commit v1 on v0

--- a/solution.py
+++ b/solution.py
@@ -141,7 +141,7 @@
         columns_all, slope_all, (((0,), (0,)), ((), ())), preferred_element_type=jnp.float32
     )
     output_total, first_bias_total, bias_total, loss_total = lax.psum(
-        (second_part, first_bias_part, bias_part, loss_part), ("dp", "seq")
+        lax.psum((second_part, first_bias_part, bias_part, loss_part), "dp"), "seq"
     )
     first_grad = lax.psum(first_shard, "dp")
     first_square = lax.psum(jnp.sum(first_grad * first_grad), "seq")

time: 935 us -> 1000 us (1.070)
  waiting for transfers between devices: 249 us -> 295 us
  blocking collectives: 212 us -> 228 us
    psum x1, waiting for transfers between devices: 0.01 us -> 45.4 us  [per_device(): first_grad = lax.psum(first_shard, 'dp')]
    psum x2, blocking collectives: 148 us -> 164 us  [the longest x1 138 us: per_device(): lax.psum(lax.psum((second_part, first_bias_part, bias_part, loss_part), '...]
  transfers between devices with their start and end apart: 4 -> 4, of which waited for: 3 -> 4; matrix products, arithmetic and copies ran while one was open for 2% -> 1% of each run, Pallas kernels for 0% -> 0%
where the time goes in v1:
time: 1000 us; the launch traced here: 988 us
  waiting for transfers between devices  295 us (30%)
  blocking collectives  228 us (23%)
  loops' own time  175 us (18%)
  other arithmetic  128 us (13%)
  local copies, waits for them, and re-layouts  92.1 us (9%)
  matrix products  52.9 us (5%)
  between operations  16.6 us (2%)
    another operation x2, loops' own time, blockwise(): return lax.fori_loop(0, rows_here // inner, visit_block, carried)  171 us
    unnamed x5, waiting for transfers between devices  165 us
    psum x1, blocking collectives, per_device(): lax.psum(lax.psum((second_part, first_bias_part, bias_part, loss_part), '...  138 us
    dynamic_slice x76, local copies, waits for them, and re-layouts, visit_block(): sub_rows = lax.dynamic_slice_in_dim(mass_portion, local_start, inner, 0)  64.7 us
    all_gather x1, waiting for transfers between devices, per_device(): keys_whole = lax.all_gather(local_key_rows, 'seq', axis=0, tiled=True)  64.1 us
    all_to_all x1, blocking collectives, per_device(): lax.all_to_all(tokens_in, 'seq', split_axis=1, concat_axis=0, tiled=True)  63.7 us
    psum x1, waiting for transfers between devices, per_device(): first_grad = lax.psum(first_shard, 'dp')  45.4 us
    reduce_min x64, other arithmetic, normalizer_step(): jnp.min(key_pos) > jnp.max(query_pos)  41.8 us
  transfers between devices with their start and end apart: 4, of which 4 were waited for; matrix products, arithmetic and copies ran while one was open for 1% of the time, Pallas kernels for 0%

profile of v1, /device:TPU:1, one launch (start us, length us, event | category | flops | bytes accessed | tf_op | source)
XLA Modules:
  0.0 987.6 jit_solution(6210191406562258500)
XLA Ops:
  11.0 64.1 %all-gather.6.cloned.1.call-done = bf16[1,4096,512]{2,1,0:T(8,128)(2,1)} async-done(((bf16[1,128,512]{2,1,0:T(8,128)(2,1)}), bf16[1,4096,512]{2,1,0:T(8,128)(2,1)}) %all-gather.6.cloned.1.call-update) | async-done | bytes 4194320 | tf_op jit(solution)/shard_map/all_gather | solution.py:107
  75.1 206.3 %while.32 = (s32[]{:T(128)}, f32[4,8,128]{2,1,0:T(8,128)S(1)}, f32[4,8,128]{2,1,0:T(8,128)S(1)}, s32[64]{0:T(128)S(1)}, s32[]{:T(128)}, /*index=5*/s32[128]{0:T(...) while((s32[]{:T(128)}, f32[4,8,128]{2,1,0:T(8,128)S(1)}, ...), condition=%wide.region_9.10_spmd, body=%wide.region_2.9_spmd.sunk | while | flops 68712320 | bytes 3713545 | solution.py:41
  87.3 1.7 conditional.4
  156.9 1.7 conditional.4
  173.1 1.7 conditional.4
  184.9 1.7 conditional.4
  199.3 1.7 conditional.4
  221.6 1.7 conditional.4
  235.6 1.7 conditional.4
  239.5 1.7 conditional.4
  269.1 1.7 conditional.4
  281.5 212.6 %while.33 = (s32[]{:T(128)}, f32[4,4096]{1,0:T(4,128)S(1)}, s32[64]{0:T(128)S(1)}, s32[]{:T(128)}, s32[128]{0:T(128)S(1)}, /*index=5*/bf16[4096,512]{1,0:T(8,128...) while((s32[]{:T(128)}, f32[4,4096]{1,0:T(4,128)S(1)}, ...), condition=%wide.region_16.17_spmd, body=%wide.region_10.16_spmd.sunk | while | flops 68441992 | bytes 1416701 | solution.py:41
  494.1 2.0 copy.51
  496.2 4.8 multiply_convert_fusion
  501.0 164.5 %reduce-scatter.4.cloned.1.call-done = f32[128,4]{1,0:T(8,128)} async-done(((f32[4096,4]{1,0:T(8,128)}), f32[128,4]{1,0:T(8,128)}) %reduce-scatter.4.cloned.1.call-update) | async-done | bytes 2064
  668.3 2.5 copy.42
  670.8 63.7 %all_to_all.19 = bf16[128,32,256]{0,2,1:T(8,128)(2,1)S(1)} all-to-all(bf16[128,32,256]{0,2,1:T(8,128)(2,1)} %bitcast.50), channel_id=1, replica_groups=mesh['dp'=8,'seq'=32] {'seq'}, dimensions={1} | all-to-all | bytes 4194304 | tf_op jit(solution)/shard_map/all_to_all | solution.py:138
  734.5 2.9 copy.43
  737.4 19.9 %all-gather.4.cloned.1.call-done = bf16[4096,512]{1,0:T(8,128)(2,1)} async-done(((bf16[128,512]{1,0:T(8,128)(2,1)}), bf16[4096,512]{1,0:T(8,128)(2,1)}) %all-gather.4.cloned.1.call-update) | async-done | bytes 4194320 | tf_op jit(solution)/shard_map/all_gather | solution.py:139
  757.3 4.9 convolution_bitcast_fusion
  763.1 26.5 %all-reduce.1 = (f32[]{:T(128)}, f32[4,512]{1,0:T(4,128)S(1)}, f32[512]{0:T(512)S(1)}, f32[4]{0:T(128)S(1)}) all-reduce(f32[]{:T(128)S(6)} %div.87, f32[4,512]{1,0:T(4,128)S(1)} %fusion.20, f32[512]{0:T(512)S(1)} %get-tuple-element.635, f32[4]{0:T(128)S(1)} %get-tuple-element.583), channel_id=1, replica_groups=mesh['dp'=8,'seq'=32] {'dp'}, use_global_device_ids=true, to_apply=%region_19.20 | all-reduce | flops 2565 | bytes 20520 | tf_op jit(solution)/shard_map/psum | solution.py:144
  789.6 45.4 %all-reduce.4.cloned.1.call-done = f32[256,512]{0,1:T(8,128)} async-done(((f32[256,512]{0,1:T(8,128)}), f32[256,512]{0,1:T(8,128)}) %all-reduce.4.cloned.1.call-update) | async-done | bytes 524304 | tf_op jit(solution)/shard_map/psum | solution.py:146
  835.0 1.8 multiply_reduce_fusion
  836.8 137.7 %all-reduce = (f32[]{:T(128)}, f32[]{:T(128)}, f32[4,512]{1,0:T(4,128)S(1)}, f32[512]{0:T(512)S(1)}, f32[4]{0:T(128)}) all-reduce(f32[]{:T(128)} %get-tuple-element.622, f32[]{:T(128)} %multiply_reduce_fusion, f32[4,512]{1,0:T(4,128)S(1)} %get-tuple-element.623, ...), channel_id=1, replica_groups=mesh['dp'=8,'seq'=32] {'seq'}, use_global_device_ids=true, to_apply=%region_20.21 | all-reduce | flops 2566 | bytes 20528 | tf_op jit(solution)/shard_map/psum | solution.py:143
  (1178 shorter events, 366.3 us)
Async XLA Ops:
  7.2 659.3 %copy-start = (bf16[4,512]{1,0:T(4,128)(2,1)S(1)}, bf16[4,512]{1,0:T(4,128)(2,1)}, u32[]{:S(2)}) copy-start(bf16[4,512]{1,0:T(4,128)(2,1)} %param.22) | copy-start | bytes 12292
  7.2 3.1 copy-start.4
  7.2 67.9 %all-gather.6.cloned.1.call-start = ((), (), s32[]{:S(2)}) async-start(), calls=%async_computation.4 | async-start | bytes 4325376 | tf_op jit(solution)/shard_map/all_gather | solution.py:107
  7.9 657.6 %reduce-scatter.4.cloned.1.call-start = ((), (), s32[]{:S(2)}) async-start(), calls=%async_computation.5 | async-start | bytes 2162688
  494.1 2.1 copy-start.1
  494.1 2.1 copy-start.2
  496.1 170.4 %copy-start.5 = (f32[4]{0:T(128)S(1)}, f32[4]{0:T(128)}, u32[]{:S(2)}) copy-start(f32[4]{0:T(128)} %param.23) | copy-start | bytes 52
  496.1 261.2 %all-gather.4.cloned.1.call-start = ((), (), s32[]{:S(2)}) async-start(), calls=%async_computation.2 | async-start | bytes 4325376 | tf_op jit(solution)/shard_map/all_gather | solution.py:139
  666.4 68.1 %copy-start.3 = (f32[4,128]{1,0:T(4,128)}, f32[4,128]{1,0:T(4,128)S(1)}, u32[]{:S(2)}) copy-start(f32[4,128]{1,0:T(4,128)S(1)} %copy.52) | copy-start | bytes 6148
  668.2 166.8 %all-reduce.4.cloned.1.call-start = ((), (), s32[]{:S(2)}) async-start(), calls=%async_computation.3 | async-start | bytes 1048576 | tf_op jit(solution)/shard_map/psum | solution.py:146
Sparse Core Ops, SparseCore 0:
  10.6 64.5 all-gather.5
  496.2 169.2 reduce-scatter.3
  668.7 88.6 all-gather.3
  762.4 72.5 all-reduce.3
